TPU v7x, 128 devices: a whole 4x4x4 slice. The times are simulated.
128 devices in a mesh: rep: 8 (over y_hi, z), fsdp: 16 (over y_lo, x, core).
Axes of the slice: x: 4, y: 4 (y_hi: 2, y_lo: 2; y = y_hi * 2 + y_lo), z: 4, core: 2. Of those that a mesh axis runs over, the one named last changes fastest.
Arguments:
- attn_out: bfloat16 [8, 4096, 2560], P('rep', 'fsdp'), may hold values from -6 to 6
- residual: bfloat16 [8, 4096, 5120], P('rep', 'fsdp'), may hold values from -400 to 400
- cotangent: bfloat16 [8, 4096, 5120], P('rep', 'fsdp'), may hold values from -2 to 2
- norm_gain: bfloat16 [5120], P('fsdp'), may hold values from 0.29882812 to 3
- params: float32 [8, 5120, 2560], P('rep', 'fsdp'), may hold values from -1 to 1
- first_moment: float32 [8, 5120, 2560], P('rep', 'fsdp'), may hold values from -3 to 3
- second_moment: float32 [8, 5120, 2560], P('rep', 'fsdp'), may hold values from 0.05 to 2
- step_count: int32 [1], replicated, may hold values from 0 to 63
Outputs:
- params_out: float32 [8, 5120, 2560], P('rep', 'fsdp')
- first_out: float32 [8, 5120, 2560], P('rep', 'fsdp')
- second_out: float32 [8, 5120, 2560], P('rep', 'fsdp')
All inputs are finite; a program needn't handle non-finite values.
Results may differ from a plain program's by a relative error of at most 0.007.
Values may be sent and summed in bfloat16 or wider, within the bound.
A program may use at most 192 MiB of HBM per device.

v0:
```python
from functools import partial

import jax
import jax.numpy as jnp
from jax import lax
from jax.sharding import PartitionSpec as P

beta_one = 0.9
beta_two = 0.999
learn_rate = 0.001
decay_rate = 0.1
norm_eps = 1e-05
adam_eps = 1e-08


def partner(value, axis, bit):
    mask = 2**bit
    pairs = [(source, source ^ mask) for source in range(lax.axis_size(axis))]
    return lax.ppermute(value, axis, pairs)


def norm_backward(pre_norm, scaled, square_sum, cross_sum, width_total):
    inv_rms = lax.rsqrt(square_sum / width_total + norm_eps)
    correction = inv_rms * inv_rms * inv_rms * cross_sum / width_total
    return (inv_rms[:, None] * scaled - pre_norm * correction[:, None]).astype(jnp.bfloat16)


def adam_change(params_local, gradient, first_local, second_local, step_count):
    step_time = (step_count[0] + 1).astype(jnp.float32)
    first_fix = 1.0 - jnp.power(jnp.float32(beta_one), step_time)
    second_fix = 1.0 - jnp.power(jnp.float32(beta_two), step_time)
    first_new = beta_one * first_local + (1.0 - beta_one) * gradient
    second_new = beta_two * second_local + (1.0 - beta_two) * gradient * gradient
    update_step = -learn_rate * (
        first_new / first_fix / (jnp.sqrt(second_new / second_fix) + adam_eps)
        + decay_rate * params_local
    )
    return (update_step, first_new, second_new)


def swap_updated(shard_data, bit_number):
    return partner(shard_data, "rep", bit_number)


def pick_partner(shard_data, partner_level, helper, level_count):
    branches = [partial(helper, bit_number=number) for number in range(level_count)]
    return lax.switch(partner_level, branches, shard_data)


def per_device(
    attn_out, residual, cotangent, norm_gain, params, first_moment, second_moment, step_count
):
    local_attn = attn_out[0]
    width_total = residual.shape[2]
    params_local = params[0]
    w_half = params_local.astype(jnp.bfloat16)
    contract_feat = (((1,), (1,)), ((), ()))
    contract_rows = (((0,), (0,)), ((), ()))
    full_attn = lax.all_gather(local_attn, "fsdp", axis=0, tiled=True)
    pre_cols = lax.dot_general(full_attn, w_half, contract_feat, preferred_element_type=jnp.float32)
    resid_cols, cotan_cols = (
        lax.all_to_all(residual[0], "fsdp", split_axis=1, concat_axis=0, tiled=True),
        lax.all_to_all(cotangent[0], "fsdp", split_axis=1, concat_axis=0, tiled=True),
    )
    pre_norm = resid_cols.astype(jnp.float32) + pre_cols
    scaled = norm_gain.astype(jnp.float32)[None, :] * cotan_cols.astype(jnp.float32)
    square_sum, cross_sum = (
        lax.psum(jnp.sum(pre_norm * pre_norm, axis=1).astype(jnp.bfloat16), "fsdp").astype(
            jnp.float32
        ),
        lax.psum(jnp.sum(pre_norm * scaled, axis=1).astype(jnp.bfloat16), "fsdp").astype(
            jnp.float32
        ),
    )
    grad_pre = norm_backward(pre_norm, scaled, square_sum, cross_sum, width_total)
    gradient = lax.dot_general(
        grad_pre, full_attn, contract_rows, preferred_element_type=jnp.float32
    )
    update_step, first_new, second_new = adam_change(
        params_local, gradient, first_moment[0], second_moment[0], step_count
    )
    level_count = lax.axis_size("rep").bit_length() - 1
    partner_level = jnp.remainder(step_count[0], level_count)
    updated = params_local + update_step
    updated_far = pick_partner(updated, partner_level, swap_updated, level_count)
    params_change = 0.5 * (updated_far - params_local) + 0.5 * update_step
    return (params_change[None], first_new[None], second_new[None])


def solution(mesh):
    return jax.shard_map(
        per_device,
        mesh=mesh,
        in_specs=(
            P("rep", "fsdp", None),
            P("rep", "fsdp", None),
            P("rep", "fsdp", None),
            P("fsdp"),
            P("rep", "fsdp", None),
            P("rep", "fsdp", None),
            P("rep", "fsdp", None),
            P(),
        ),
        out_specs=(P("rep", "fsdp", None), P("rep", "fsdp", None), P("rep", "fsdp", None)),
        check_vma=False,
    )
```

profile of v0, /device:TPU:1, one launch (start us, length us, event | category | flops | bytes accessed | tf_op | source)
XLA Modules:
  0.0 359.7 jit_solution(13053667947359435022)
XLA Ops:
  7.2 0.0 all-gather.3.cloned.1.call-start
  7.2 0.7 all-gather.3.cloned.1.call-update
  7.9 4.4 %copy.13 = bf16[1,256,5120]{1,2,0:T(8,128)(2,1)} copy(bf16[1,256,5120]{2,1,0:T(8,128)(2,1)} %param.12) | data formatting | bytes 5242880 | tf_op args[1]
  12.3 6.8 %all-to-all-start = ((bf16[256,16,320]{0,2,1:T(8,128)(2,1)}), bf16[256,16,320]{0,2,1:T(8,128)(2,1)S(1)}, u32[]{:S(2)}, u32[]{:S(2)}) async-start(bf16[256,16,320]{0,2,1:T(8,128)(2,1)} %bitcast.3), calls=%async_computation | async-start | bytes 5242880 | tf_op jit(solution)/shard_map/all_to_all | solution.py:62
  19.1 4.4 %copy.15 = bf16[1,256,5120]{1,2,0:T(8,128)(2,1)} copy(bf16[1,256,5120]{2,1,0:T(8,128)(2,1)} %param.13) | data formatting | bytes 5242880 | tf_op args[2]
  23.5 0.0 copy-start.1
  23.5 53.0 %all-to-all-done = bf16[256,16,320]{0,2,1:T(8,128)(2,1)S(1)} async-done(((bf16[256,16,320]{0,2,1:T(8,128)(2,1)}), bf16[256,16,320]{0,2,1:T(8,128)(2,1)S(1)}, u32[]{:S(2)}, u32[]{:S(2)}) %all-to-all-start) | async-done | bytes 2621472 | tf_op jit(solution)/shard_map/all_to_all | solution.py:62
  76.5 5.1 %all-to-all-start.1 = ((bf16[256,16,320]{0,2,1:T(8,128)(2,1)}), bf16[256,16,320]{0,2,1:T(8,128)(2,1)}, u32[]{:S(2)}, u32[]{:S(2)}) async-start(bf16[256,16,320]{0,2,1:T(8,128)(2,1)} %bitcast.6), calls=%async_computation.1 | async-start | bytes 5242880 | tf_op jit(solution)/shard_map/all_to_all | solution.py:63
  82.3 0.0 copy-done.1
  82.3 0.6 convert_bitcast_fusion.1
  82.9 3.0 copy.17
  85.9 55.5 %all-to-all-done.1 = bf16[256,16,320]{0,2,1:T(8,128)(2,1)} async-done(((bf16[256,16,320]{0,2,1:T(8,128)(2,1)}), bf16[256,16,320]{0,2,1:T(8,128)(2,1)}, u32[]{:S(2)}, u32[]{:S(2)}) %all-to-all-start.1) | async-done | bytes 2621472 | tf_op jit(solution)/shard_map/all_to_all | solution.py:63
  141.4 2.4 convert_bitcast_fusion
  143.8 0.0 copy-start
  143.8 2.9 copy.18
  146.8 31.8 %all-gather.3.cloned.1.call-done = bf16[1,4096,2560]{2,1,0:T(8,128)(2,1)} async-done(((bf16[1,256,2560]{2,1,0:T(8,128)(2,1)}), bf16[1,4096,2560]{2,1,0:T(8,128)(2,1)}) %all-gather.3.cloned.1.call-update) | async-done | bytes 20971536 | tf_op jit(solution)/shard_map/all_gather | solution.py:59
  178.6 0.0 copy-done
  178.6 24.1 %multiply_reduce_fusion.1 = (bf16[4096]{0:T(1024)(128)(2,1)S(1)}, bf16[4096]{0:T(1024)(128)(2,1)S(1)}, f32[4096,320]{0,1:T(8,128)}) fusion(f32[4096,320]{0,1:T(8,128)} %bitcast.77, f32[320]{0:T(512)S(1)} %convert_element_type.49, f32[4096,320]{0,1:T(8,128)} %bitcast.79, bf16[1,4096,2560]{2,1,0:T(8,128)(2,1)} %all-gather.3.cloned.1.call-done, ...), kind=kOutput, calls=%fused_computation.9 | convolution fusion | flops 6718742528 | bytes 39994624 | tf_op jit(solution)/shard_map/dot_general | solution.py:60
  202.7 51.1 %all-reduce = (bf16[4096]{0:T(1024)(128)(2,1)S(1)}, bf16[4096]{0:T(1024)(128)(2,1)S(1)}) all-reduce(bf16[4096]{0:T(1024)(128)(2,1)S(1)} %get-tuple-element.11, bf16[4096]{0:T(1024)(128)(2,1)S(1)} %get-tuple-element.10), channel_id=1, replica_groups=mesh['rep'=8,'fsdp'=16] {'fsdp'}, use_global_device_ids=true, to_apply=%region_3.0 | all-reduce | flops 8192 | bytes 32768 | tf_op jit(solution)/shard_map/psum | solution.py:71
  253.8 19.5 %bitcast_add_fusion.1 = (f32[320,2560]{1,0:T(8,128)}, f32[320,2560]{1,0:T(8,128)}) fusion(f32[1,320,2560]{2,1,0:T(8,128)S(1)} %copy-done, f32[]{:T(128)} %bitcast.10, f32[1,320,2560]{2,1,0:T(8,128)} %param.17, f32[]{:T(128)} %bitcast.8, f32[1,320,2560]{2,1,0:T(8,128)} %param.16, bf16[1,4096,2560]{2,1,0:T(8,128)(2,1)} %all-gather.3.cloned.1.call-done, ...), kind=kOutput, calls=%fused_computation.14 | convolution fusion | flops 6729728000 | bytes 47875336 | tf_op jit(solution)/shard_map/dot_general | solution.py:76
  273.3 70.8 %conditional.1 = (f32[320,2560]{1,0:T(8,128)}) conditional(s32[]{:T(128)} %clamp.3, f32[320,2560]{1,0:T(8,128)} %get-tuple-element.20, f32[320,2560]{1,0:T(8,128)} %get-tuple-element.20, f32[320,2560]{1,0:T(8,128)} %get-tuple-element.20), branch_computations={%region_4.5_spmd, %region_5.6_spmd, %region_6.7_spmd} | conditional | bytes 13107248 | solution.py:47
  273.3 3.7 %collective-permute-start.1 = (f32[320,2560]{1,0:T(8,128)}, f32[320,2560]{1,0:T(8,128)}, u32[]{:S(2)}, u32[]{:S(2)}) collective-permute-start(f32[320,2560]{1,0:T(8,128)} %param.1), channel_id=1, source_target_pairs={{0,32},{16,48},{32,0},{48,16},{64,96},{80,112},{96,64},{112,80},{1... | collective-permute-start | bytes 9830408 | tf_op jit(solution)/shard_map/cond/branch_1_fun/ppermute | solution.py:19
  277.0 67.2 %collective-permute-done.1 = f32[320,2560]{1,0:T(8,128)} collective-permute-done((f32[320,2560]{1,0:T(8,128)}, f32[320,2560]{1,0:T(8,128)}, u32[]{:S(2)}, u32[]{:S(2)}) %collective-permute-start.1) | collective-permute-done | bytes 3276832 | tf_op jit(solution)/shard_map/cond/branch_1_fun/ppermute | solution.py:19
  344.1 8.7 %fusion.16 = (f32[1,320,2560]{2,1,0:T(8,128)}, f32[1,320,2560]{2,1,0:T(8,128)}, f32[1,320,2560]{2,1,0:T(8,128)}) fusion(f32[320,2560]{1,0:T(8,128)} %get-tuple-element.21, f32[1,320,2560]{2,1,0:T(8,128)} %param.17, f32[]{:T(128)} %bitcast.10, f32[]{:T(128)} %bitcast.8, f32[1,320,2560]{2,1,0:T(8,128)} %param.16, f32[320,2560]{1,0:T(8,128)} %get-tuple-element.22, ...), kind=kLoop, calls=%fused_computation.25 | loop fusion | flops 13926400 | bytes 26214408 | tf_op jit(solution)/shard_map/broadcast_in_dim | solution.py:87
  (2 shorter events, 0.0 us)
Async XLA Ops:
  7.2 171.5 %all-gather.3.cloned.1.call-start = ((), (), s32[]{:S(2)}) async-start(), calls=%async_computation.2 | async-start | bytes 22282240 | tf_op jit(solution)/shard_map/all_gather | solution.py:59
  12.3 64.2 %all-to-all-start = ((bf16[256,16,320]{0,2,1:T(8,128)(2,1)}), bf16[256,16,320]{0,2,1:T(8,128)(2,1)S(1)}, u32[]{:S(2)}, u32[]{:S(2)}) async-start(bf16[256,16,320]{0,2,1:T(8,128)(2,1)} %bitcast.3), calls=%async_computation | async-start | bytes 5242880 | tf_op jit(solution)/shard_map/all_to_all | solution.py:62
  23.5 58.8 %copy-start.1 = (bf16[320]{0:T(512)(128)(2,1)S(1)}, bf16[320]{0:T(512)(128)(2,1)}, u32[]{:S(2)}) copy-start(bf16[320]{0:T(512)(128)(2,1)} %param.14) | copy-start | bytes 1924
  76.5 64.9 %all-to-all-start.1 = ((bf16[256,16,320]{0,2,1:T(8,128)(2,1)}), bf16[256,16,320]{0,2,1:T(8,128)(2,1)}, u32[]{:S(2)}, u32[]{:S(2)}) async-start(bf16[256,16,320]{0,2,1:T(8,128)(2,1)} %bitcast.6), calls=%async_computation.1 | async-start | bytes 5242880 | tf_op jit(solution)/shard_map/all_to_all | solution.py:63
  143.8 34.8 %copy-start = (f32[1,320,2560]{2,1,0:T(8,128)S(1)}, f32[1,320,2560]{2,1,0:T(8,128)}, u32[]{:S(2)}) copy-start(f32[1,320,2560]{2,1,0:T(8,128)} %param.15) | copy-start | bytes 9830404
  273.3 70.8 %collective-permute-start.1 = (f32[320,2560]{1,0:T(8,128)}, f32[320,2560]{1,0:T(8,128)}, u32[]{:S(2)}, u32[]{:S(2)}) collective-permute-start(f32[320,2560]{1,0:T(8,128)} %param.1), channel_id=1, source_target_pairs={{0,32},{16,48},{32,0},{48,16},{64,96},{80,112},{96,64},{112,80},{1... | collective-permute-start | bytes 9830408 | tf_op jit(solution)/shard_map/cond/branch_1_fun/ppermute | solution.py:19
Sparse Core Ops, SparseCore 0:
  9.7 168.8 all-gather.2
where the time goes:
time: 364 us; the launch traced here: 360 us
  waiting for transfers between devices  208 us (57%)
  blocking collectives  51.1 us (14%)
  matrix products  43.6 us (12%)
  starting transfers between devices  15.6 us (4%)
  between operations  14.8 us (4%)
  local copies, waits for them, and re-layouts  14.7 us (4%)
  other arithmetic  11.8 us (3%)
    ppermute x1, waiting for transfers between devices, partner(): return lax.ppermute(value, axis, pairs)  67.2 us
    all_to_all x1, waiting for transfers between devices, per_device(): lax.all_to_all(cotangent[0], 'fsdp', split_axis=1, concat_axis=0, tiled=T...  55.5 us
    all_to_all x1, waiting for transfers between devices, per_device(): lax.all_to_all(residual[0], 'fsdp', split_axis=1, concat_axis=0, tiled=True)  53 us
    psum x1, blocking collectives, per_device(): lax.psum(jnp.sum(pre_norm * scaled, axis=1).astype(jnp.bfloat16), 'fsdp')  51.1 us
    all_gather x1, waiting for transfers between devices, per_device(): full_attn = lax.all_gather(local_attn, 'fsdp', axis=0, tiled=True)  31.8 us
    dot_general x1, matrix products, per_device(): lax.dot_general(full_attn, w_half, contract_feat, preferred_element_type=...  24.1 us
    dot_general x1, matrix products, per_device(): lax.dot_general(grad_pre, full_attn, contract_rows, preferred_element_typ...  19.5 us
    unnamed x6, local copies, waits for them, and re-layouts  8.76 us
  transfers between devices with their start and end apart: 4, of which 4 were waited for; matrix products, arithmetic and copies ran while one was open for 5% of the time, Pallas kernels for 0%

commit v1 on v0

v1 whole, which is shorter than its diff:
```python
import functools

import jax
import jax.numpy as jnp
from jax import lax
from jax.experimental import pallas as pl
from jax.experimental.pallas import tpu as pltpu
from jax.sharding import PartitionSpec as P

beta_one = 0.9
beta_two = 0.999
learn_rate = 0.001
decay_rate = 0.1
norm_eps = 1e-05
adam_eps = 1e-08

MESH = pl.DeviceIdType.MESH
N_X = 4
N_ROW = 2 * N_X
N_PH = 4


def remote(src, dst, send_sem, recv_sem, device):
    return pltpu.make_async_remote_copy(
        src_ref=src,
        dst_ref=dst,
        send_sem=send_sem,
        recv_sem=recv_sem,
        device_id=device,
        device_id_type=MESH,
    )


def step_kernel(
    bit,
    attn, resid, cotan, gain_in, params, first_in, second_in, fixes,
    params_out, first_out, second_out,
    attn_v, res_v, cot_v, w_v, w_s, gain_r, pre_v, gp_v, acc, sums_v, inv_v, cor_v, st_s, st_r,
    gs_v, near_v, far_v, p_v, pf_v, m_v, v_v, us_v, uf_v,
    own_sem, loc_sem, attn_ss, attn_rs, fwd_ss, rel_ss, a2a_ss, a2a_rs, w_ss, w_rs, g_ss, g_rs,
    pf_ss, pf_rs, st_ss, st_rs, far_ss, far_rs, near_ss, near_rs, u_ss, u_rs, out_sem,
):
    tokens = attn.shape[1]
    piece = tokens // N_PH
    half = piece // 2
    pair = N_ROW * piece
    width = resid.shape[2]
    shard = params.shape[1]
    feats = 2 * shard
    n_chunk, _, chunk = acc.shape

    rep = lax.axis_index("rep")
    me = lax.axis_index("fsdp")
    y = lax.div(me, N_ROW)
    idx = lax.rem(me, N_ROW)
    x = lax.div(idx, 2)
    c = lax.rem(idx, 2)
    oc = 1 - c
    oy = 1 - y
    keeper = c == y
    chips = (x, lax.rem(x + 1, N_X), lax.rem(x + N_X - 1, N_X), lax.rem(x + 2, N_X))
    mirror = (0, 2, 1, 3)

    def dev(yy, xx, cc):
        return (rep, yy * N_ROW + xx * 2 + cc)

    m = 1 << bit
    peer = (rep + m * (1 - 2 * lax.rem(lax.div(rep, m), 2)), me)
    right, left, other = dev(y, chips[1], c), dev(y, chips[2], c), dev(y, x, oc)
    row_peers = [(rep, y * N_ROW + lax.rem(idx + k, N_ROW)) for k in range(1, N_ROW)]
    greet = row_peers + [dev(oy, x, 0), dev(oy, x, 1), peer]

    def rows(s, chip, core, part=None):
        start = s * pair + (chip * 2 + core) * piece
        if part is None:
            return pl.ds(pl.multiple_of(start, piece), piece)
        return pl.ds(pl.multiple_of(start + part * half, half), half)

    def cols(chip, core):
        return pl.ds(pl.multiple_of((core * N_X + chip) * feats, feats), feats)

    def own_load(s, which):
        src = pl.ds(s * piece, piece)
        if which == 2:
            return pltpu.make_async_copy(
                attn.at[0, src], attn_v.at[rows(s, x, c)], own_sem.at[s, which]
            )
        source, target = ((resid, res_v), (cotan, cot_v))[which]
        return pltpu.make_async_copy(
            source.at[0, src, cols(x, c)], target.at[rows(s, x, c)], own_sem.at[s, which]
        )

    load_p = pltpu.make_async_copy(params.at[0], p_v, loc_sem.at[0])
    load_m = pltpu.make_async_copy(first_in.at[0], m_v, loc_sem.at[1])
    load_v = pltpu.make_async_copy(second_in.at[0], v_v, loc_sem.at[2])
    load_p.start()

    barrier = pltpu.get_barrier_semaphore()
    for device in greet:
        pl.semaphore_signal(barrier, inc=1, device_id=device, device_id_type=MESH)
    pl.semaphore_wait(barrier, len(greet))

    def tokens_copy(s, order):
        place, device = ((2, right), (1, left), (0, other))[order]
        return remote(
            attn.at[0, pl.ds(s * piece, piece)],
            attn_v.at[rows(s, x, c)],
            attn_ss.at[s, order],
            attn_rs.at[s, place, 0 if place else 1, 0],
            device,
        )

    def features_copy(s, place, rel, which):
        chip, core = chips[mirror[place]], oc if rel else c
        source, target = ((resid, res_v), (cotan, cot_v))[which]
        return remote(
            source.at[0, pl.ds(s * piece, piece), cols(chip, core)],
            target.at[rows(s, x, c)],
            a2a_ss.at[s, place, rel, which],
            a2a_rs.at[s, place, rel, which],
            dev(y, chip, core),
        )

    routes = [
        (place, rel, which)
        for place in (2, 1, 3, 0)
        for rel in range(2)
        for which in range(2)
        if place or rel
    ]

    def send_tokens(s):
        for order in range(3):
            tokens_copy(s, order).start()
        own_load(s, 2).start()

    def send_features(s):
        for route in routes:
            features_copy(s, *route).start()
        own_load(s, 0).start()
        own_load(s, 1).start()

    send_tokens(0)
    send_tokens(1)
    send_features(0)
    pf_copy = remote(params.at[0], pf_v, pf_ss, pf_rs, peer)
    pf_copy.start()

    load_p.wait()
    step = 64 if shard % 64 == 0 else shard

    @pl.loop(0, shard // step)
    def _(i):
        r = pl.ds(pl.multiple_of(i * step, step), step)
        w_s[r, :] = p_v[r, :].astype(jnp.bfloat16)

    own_w = pl.ds(pl.multiple_of(c * shard, shard), shard)
    w_far = remote(w_s, w_v.at[own_w], w_ss.at[0], w_rs.at[c], dev(oy, x, y))
    g_far = remote(gain_in, gain_r.at[c], g_ss.at[0], g_rs.at[c], dev(oy, x, y))
    w_near = remote(w_s, w_v.at[own_w], w_ss.at[1], w_rs.at[c], other)
    g_near = remote(gain_in, gain_r.at[c], g_ss.at[1], g_rs.at[c], other)
    w_far.start()
    g_far.start()

    @pl.when(jnp.logical_not(keeper))
    def _():
        w_near.start()
        g_near.start()

    @pl.when(keeper)
    def _():
        gain_r[c] = gain_in[...]

        @pl.loop(0, shard // step)
        def _(i):
            r = pl.ds(pl.multiple_of(i * step, step), step)
            d = pl.ds(pl.multiple_of(c * shard + i * step, step), step)
            w_v[d, :] = w_s[r, :]

    load_m.start()
    load_v.start()

    @pl.loop(0, n_chunk)
    def _(j):
        acc[j] = jnp.zeros(acc.shape[1:], jnp.float32)

    def arrival(s, place, rel, part=None):
        dst = attn_v.at[rows(s, chips[place], oc if rel else c, part)]
        n = part or 0
        return remote(dst, dst, fwd_ss.at[s, place, n], attn_rs.at[s, place, rel, n], other)

    def forward(s, place, part=None):
        dst = attn_v.at[rows(s, chips[place], c, part)]
        n = part or 0
        return remote(dst, dst, fwd_ss.at[s, place, n], attn_rs.at[s, place, 1, n], other)

    def relay(s, part):
        place, device = ((2, right), (1, left))[part]
        dst = attn_v.at[rows(s, chips[place], c, part)]
        return remote(dst, dst, rel_ss.at[s, part], attn_rs.at[s, 3, 0, part], device)

    def issue(s):
        arrival(s, 2, 0).wait_recv()
        relay(s, 0).start()
        arrival(s, 1, 0).wait_recv()
        relay(s, 1).start()
        forward(s, 1).start()
        forward(s, 2).start()
        if s + 2 < N_PH:
            send_tokens(s + 2)
            send_features(s + 1)
        elif s + 1 == N_PH:
            send_features(s)

    issue(0)

    def w_arrival(core):
        return remote(
            w_s, w_v.at[pl.ds(core * shard, shard)], w_ss.at[0], w_rs.at[core], other
        )

    def g_arrival(core):
        return remote(gain_in, gain_r.at[core], g_ss.at[0], g_rs.at[core], other)

    lane = lax.broadcasted_iota(jnp.int32, (64, 128), 1)

    def st_copy(t, k):
        return remote(
            st_s.at[t], st_r.at[t, k], st_ss.at[t, k], st_rs.at[t, k], row_peers[k - 1]
        )

    def far_copy(j, core):
        return remote(
            gs_v.at[j, pl.ds(core * shard, shard)],
            far_v.at[j],
            far_ss.at[j, core],
            far_rs.at[j],
            dev(oy, x, core),
        )

    def near_copy(j):
        return remote(
            acc.at[j, pl.ds(pl.multiple_of(oc * shard, shard), shard)],
            near_v.at[j],
            near_ss.at[j],
            near_rs.at[j],
            other,
        )

    @pl.loop(0, N_PH)
    def _(t):
        for s in range(N_PH):

            @pl.when(t == s)
            def _():
                if s + 1 < N_PH:
                    issue(s + 1)
                own_load(s, 2).wait()
                arrival(s, 0, 1).wait_recv()
                arrival(s, 1, 1).wait_recv()
                arrival(s, 2, 1).wait_recv()
                for part in range(2):
                    arrival(s, 3, 0, part).wait_recv()
                    forward(s, 3, part).start()
                for part in range(2):
                    arrival(s, 3, 1, part).wait_recv()

        @pl.when(t == 0)
        def _():
            for core in range(2):

                @pl.when(jnp.logical_or(jnp.logical_not(keeper), c != core))
                def _():
                    w_arrival(core).wait_recv()
                    g_arrival(core).wait_recv()

        base = pl.multiple_of(t * pair, pair)
        pre_v[...] = lax.dot_general(
            attn_v[pl.ds(base, pair), :],
            w_v[...],
            (((1,), (1,)), ((), ())),
            preferred_element_type=jnp.float32,
        )

        for s in range(N_PH):

            @pl.when(t == s)
            def _():
                own_load(s, 0).wait()
                own_load(s, 1).wait()
                for place, rel, which in routes:
                    block = (res_v, cot_v)[which].at[rows(s, chips[place], oc if rel else c)]
                    remote(
                        block,
                        block,
                        a2a_ss.at[s, place, rel, which],
                        a2a_rs.at[s, place, rel, which],
                        other,
                    ).wait_recv()

        gain = gain_r[0, 0:1, :] + gain_r[1, 0:1, :]

        @pl.loop(0, pair // 64)
        def _(i):
            r = pl.ds(pl.multiple_of(i * 64, 64), 64)
            b = pl.ds(pl.multiple_of(base + i * 64, 64), 64)
            pre = pre_v[r, :] + res_v[b, :].astype(jnp.float32)
            pre_v[r, :] = pre
            scaled = gain * cot_v[b, :].astype(jnp.float32)
            square = jnp.sum(pre * pre, axis=1, keepdims=True)
            cross = jnp.sum(pre * scaled, axis=1, keepdims=True)
            sums_v[r, :] = jnp.where(lane == 0, square, cross)

        part_sums = sums_v[...].T[0:2, :]
        st_s[t] = part_sums
        for k in range(1, N_ROW):
            st_copy(t, k).start()
        total = part_sums
        for k in range(1, N_ROW):
            st_copy(t, k).wait_recv()
            total = total + st_r[t, k]
        inv_rms = lax.rsqrt(total[0:1, :] / width + norm_eps)
        correction = inv_rms * inv_rms * inv_rms * total[1:2, :] / width
        inv_v[...] = jnp.broadcast_to(inv_rms, (128, pair)).T
        cor_v[...] = jnp.broadcast_to(correction, (128, pair)).T

        sub = min(128, pair)

        @pl.loop(0, pair // sub)
        def _(i):
            r = pl.ds(pl.multiple_of(i * sub, sub), sub)
            b = pl.ds(pl.multiple_of(base + i * sub, sub), sub)
            inv, cor = inv_v[r, :], cor_v[r, :]
            for k in range(feats // 128):
                f = slice(k * 128, (k + 1) * 128)
                scaled = gain[:, f] * cot_v[b, f].astype(jnp.float32)
                grad_pre = (inv * scaled - pre_v[r, f] * cor).astype(jnp.bfloat16)
                gp_v[f, r] = grad_pre.T

        @pl.loop(0, n_chunk)
        def _(j):
            q = pl.ds(pl.multiple_of(j * chunk, chunk), chunk)
            acc[j] += jnp.dot(
                gp_v[...], attn_v[pl.ds(base, pair), q], preferred_element_type=jnp.float32
            )

            @pl.when(jnp.logical_and(t == N_PH - 1, keeper))
            def _():
                near_copy(j).start()

            @pl.when(jnp.logical_and(t == N_PH - 1, jnp.logical_not(keeper)))
            def _():
                gs_v[j] = acc[j].astype(jnp.bfloat16)
                far_copy(j, 0).start()
                far_copy(j, 1).start()

    load_m.wait()
    load_v.wait()
    pf_copy.wait_recv()
    first_fix, second_fix = fixes[0], fixes[1]

    def u_copy(j):
        return remote(us_v.at[j], uf_v.at[j], u_ss.at[j], u_rs.at[j], peer)

    def out_copy(which, src, dst, j):
        q = pl.ds(pl.multiple_of(j * chunk, chunk), chunk)
        return pltpu.make_async_copy(src.at[:, q], dst.at[0, :, q], out_sem.at[which, j])

    def finish(j):
        q = pl.ds(pl.multiple_of(j * chunk, chunk), chunk)
        u_copy(j).wait_recv()

        @pl.loop(0, shard // step)
        def _(i):
            r = pl.ds(pl.multiple_of(i * step, step), step)
            p_v[r, q] = pf_v[r, q] + 0.5 * uf_v[j, r, :].astype(jnp.float32)

        out_copy(0, p_v, params_out, j).start()

    lag = min(2, n_chunk)

    @pl.loop(0, n_chunk)
    def _(j):
        q = pl.ds(pl.multiple_of(j * chunk, chunk), chunk)

        @pl.when(keeper)
        def _():
            near_v[j] = acc[j, pl.ds(pl.multiple_of(c * shard, shard), shard), :]

        @pl.when(jnp.logical_not(keeper))
        def _():
            near_copy(j).wait_recv()

        far_copy(j, 0).wait_recv()

        @pl.loop(0, shard // step)
        def _(i):
            r = pl.ds(pl.multiple_of(i * step, step), step)
            gradient = near_v[j, r, :] + far_v[j, r, :].astype(jnp.float32)
            p = p_v[r, q]
            first_new = beta_one * m_v[r, q] + (1.0 - beta_one) * gradient
            second_new = beta_two * v_v[r, q] + (1.0 - beta_two) * gradient * gradient
            m_v[r, q] = first_new
            v_v[r, q] = second_new
            update = -learn_rate * (
                first_new * first_fix / (jnp.sqrt(second_new * second_fix) + adam_eps)
                + decay_rate * p
            )
            us_v[j, r, :] = update.astype(jnp.bfloat16)
            pf_v[r, q] = 0.5 * (pf_v[r, q] - p) + 0.5 * update

        u_copy(j).start()
        out_copy(1, m_v, first_out, j).start()
        out_copy(2, v_v, second_out, j).start()

        @pl.when(j >= lag)
        def _():
            finish(j - lag)

    @pl.loop(n_chunk - lag, n_chunk)
    def _(j):
        finish(j)

    for s in range(N_PH):
        for order in range(3):
            tokens_copy(s, order).wait_send()
        for route in routes:
            features_copy(s, *route).wait_send()
        for part in range(2):
            relay(s, part).wait_send()
            forward(s, 3, part).wait_send()
        forward(s, 1).wait_send()
        forward(s, 2).wait_send()
    pf_copy.wait_send()
    w_far.wait_send()
    g_far.wait_send()

    @pl.when(jnp.logical_not(keeper))
    def _():
        w_near.wait_send()
        g_near.wait_send()

    @pl.loop(0, N_PH)
    def _(t):
        for k in range(1, N_ROW):
            st_copy(t, k).wait_send()

    @pl.loop(0, n_chunk)
    def _(j):
        @pl.when(keeper)
        def _():
            near_copy(j).wait_send()

        @pl.when(jnp.logical_not(keeper))
        def _():
            far_copy(j, 0).wait_send()
            far_copy(j, 1).wait_send()

        u_copy(j).wait_send()
        out_copy(0, p_v, params_out, j).wait()
        out_copy(1, m_v, first_out, j).wait()
        out_copy(2, v_v, second_out, j).wait()


def run_step(attn, resid, cotan, gain_in, params, first, second, fixes, *, bit):
    tokens, heads = attn.shape[1:]
    shard = params.shape[1]
    feats, row = 2 * shard, N_ROW * tokens
    pair = row // N_PH
    chunk = 256 if heads % 256 == 0 and heads > 256 else 128
    n_chunk = heads // chunk
    bf16, f32, dma = jnp.bfloat16, jnp.float32, pltpu.SemaphoreType.DMA
    any_spec = pl.BlockSpec(memory_space=pl.ANY)
    vmem = pltpu.VMEM
    out = jax.ShapeDtypeStruct(params.shape, f32)
    return pl.pallas_call(
        functools.partial(step_kernel, bit),
        out_shape=(out, out, out),
        in_specs=[
            any_spec,
            any_spec,
            any_spec,
            pl.BlockSpec(memory_space=pltpu.VMEM),
            any_spec,
            any_spec,
            any_spec,
            pl.BlockSpec(memory_space=pltpu.SMEM),
        ],
        out_specs=(any_spec, any_spec, any_spec),
        scratch_shapes=[
            vmem((row, heads), bf16),
            vmem((row, feats), bf16),
            vmem((row, feats), bf16),
            vmem((feats, heads), bf16),
            vmem((shard, heads), bf16),
            vmem((2, 8, feats), f32),
            vmem((pair, feats), f32),
            vmem((feats, pair), bf16),
            vmem((n_chunk, feats, chunk), f32),
            vmem((pair, 128), f32),
            vmem((pair, 128), f32),
            vmem((pair, 128), f32),
            vmem((N_PH, 2, pair), f32),
            vmem((N_PH, N_ROW, 2, pair), f32),
            vmem((n_chunk, feats, chunk), bf16),
            vmem((n_chunk, shard, chunk), f32),
            vmem((n_chunk, shard, chunk), bf16),
            vmem((shard, heads), f32),
            vmem((shard, heads), f32),
            vmem((shard, heads), f32),
            vmem((shard, heads), f32),
            vmem((n_chunk, shard, chunk), bf16),
            vmem((n_chunk, shard, chunk), bf16),
            dma((N_PH, 3)),
            dma((3,)),
            dma((N_PH, 3)),
            dma((N_PH, 4, 2, 2)),
            dma((N_PH, 4, 2)),
            dma((N_PH, 2)),
            dma((N_PH, 4, 2, 2)),
            dma((N_PH, 4, 2, 2)),
            dma((2,)),
            dma((2,)),
            dma((2,)),
            dma((2,)),
            dma,
            dma,
            dma((N_PH, N_ROW)),
            dma((N_PH, N_ROW)),
            dma((n_chunk, 2)),
            dma((n_chunk,)),
            dma((n_chunk,)),
            dma((n_chunk,)),
            dma((n_chunk,)),
            dma((n_chunk,)),
            dma((3, n_chunk)),
        ],
        compiler_params=pltpu.CompilerParams(
            collective_id=bit,
            has_side_effects=True,
            vmem_limit_bytes=63 * 2**20,
        ),
        name=f"step_{bit}",
    )(attn, resid, cotan, gain_in, params, first, second, fixes)


def per_device(attn_out, residual, cotangent, norm_gain, params, first, second, step_count):
    step_time = (step_count[0] + 1).astype(jnp.float32)
    first_fix = 1.0 - jnp.power(jnp.float32(beta_one), step_time)
    second_fix = 1.0 - jnp.power(jnp.float32(beta_two), step_time)
    fixes = jnp.stack([1.0 / first_fix, 1.0 / second_fix])
    shard = norm_gain.shape[0]
    core = lax.rem(lax.axis_index("fsdp"), 2)
    gain = norm_gain.astype(jnp.float32)
    owner = lax.div(lax.broadcasted_iota(jnp.int32, (8, 2 * shard), 1), shard)
    gain_in = jnp.where(owner == core, jnp.concatenate([gain, gain])[None, :], 0.0)
    level_count = lax.axis_size("rep").bit_length() - 1
    level = jnp.remainder(step_count[0], level_count)
    branches = [functools.partial(run_step, bit=bit) for bit in range(level_count)]
    return lax.switch(
        level, branches, attn_out, residual, cotangent, gain_in, params, first, second, fixes
    )


def solution(mesh):
    split = P("rep", "fsdp", None)
    return jax.shard_map(
        per_device,
        mesh=mesh,
        in_specs=(split, split, split, P("fsdp"), split, split, split, P()),
        out_specs=(split, split, split),
        check_vma=False,
    )
```

time: 364 us -> 262 us (0.72); the launches traced: 360 us -> 261 us
  Pallas kernels: 0 us -> 249 us
  waiting for transfers between devices: 208 us -> 0 us
  blocking collectives: 51.1 us -> 0 us
  matrix products: 43.6 us -> 0 us
  starting transfers between devices: 15.6 us -> 0 us
  between operations: 14.8 us -> 1.48 us
  other arithmetic: 11.8 us -> 1.53 us
  local copies, waits for them, and re-layouts: 14.7 us -> 8.83 us
    pallas_call x0 -> x1, Pallas kernels: none -> 249 us  [run_step(): pl.pallas_call(functools.partial(step_kernel, bit), out_shape=(out, out,...]
    all_to_all x2 -> x0, waiting for transfers between devices: 108 us -> none  [the longest x1 55.5 us: per_device(): lax.all_to_all(cotangent[0], 'fsdp', split_axis=1, concat_axis=0, tiled=T...]
    ppermute x1 -> x0, waiting for transfers between devices: 67.2 us -> none  [partner(): return lax.ppermute(value, axis, pairs)]
    psum x1 -> x0, blocking collectives: 51.1 us -> none  [per_device(): lax.psum(jnp.sum(pre_norm * scaled, axis=1).astype(jnp.bfloat16), 'fsdp')]
    dot_general x2 -> x0, matrix products: 43.6 us -> none  [the longest x1 24.1 us: per_device(): lax.dot_general(full_attn, w_half, contract_feat, preferred_element_type=...]
    all_gather x1 -> x0, waiting for transfers between devices: 31.8 us -> none  [per_device(): full_attn = lax.all_gather(local_attn, 'fsdp', axis=0, tiled=True)]
    all_to_all x2 -> x0, starting transfers between devices: 11.9 us -> none  [the longest x1 6.82 us: per_device(): lax.all_to_all(residual[0], 'fsdp', split_axis=1, concat_axis=0, tiled=True)]
    broadcast_in_dim x1 -> x0, other arithmetic: 8.74 us -> none  [per_device(): return (params_change[None], first_new[None], second_new[None])]
  transfers between devices with their start and end apart: 4 -> 0, of which waited for: 4 -> 0; matrix products, arithmetic and copies ran while one was open for 5% -> 0% of each run, Pallas kernels for 0% -> 0%
where the time goes in v1:
time: 262 us; the launch traced here: 261 us
  Pallas kernels  249 us (95%)
  local copies, waits for them, and re-layouts  8.83 us (3%)
    pallas_call x1, Pallas kernels, run_step(): pl.pallas_call(functools.partial(step_kernel, bit), out_shape=(out, out,...  249 us
    unnamed x7, local copies, waits for them, and re-layouts  8.82 us

profile of v1, /device:TPU:1, one launch (start us, length us, event | category | flops | bytes accessed | tf_op | source)
XLA Modules:
  0.0 261.5 jit_solution(11639704031919857411)
XLA Ops:
  1.5 0.1 pad_maximum_fusion
  1.5 0.8 maximum_convert_fusion
  2.4 250.3 %conditional.1 = ((f32[1,320,2560]{2,1,0:T(8,128)}, f32[1,320,2560]{2,1,0:T(8,128)}, f32[1,320,2560]{2,1,0:T(8,128)})) conditional(s32[]{:T(128)} %clamp.3, (bf16[1,256,2560]{2,1,0:T(8,128)(2,1)}, bf16[1,256,5120]{2,1,0:T(8,128)(2,1)}, bf16[1,256,5120]{2,1,0:T(8,128)(2,1)}, s32[640]{0:T(1024)S(1)}, ...), branch_computations={%region_0.1_spmd.clone, %region_1.2_spmd.clone, %region_2.3_spmd.c... | conditional | flops 6402 | bytes 26913 | solution.py:560
  2.4 0.6 broadcast_select_fusion.2.gain_in
  3.0 249.4 %step_2.1 = (f32[1,320,2560]{2,1,0:T(8,128)}, f32[1,320,2560]{2,1,0:T(8,128)}, f32[1,320,2560]{2,1,0:T(8,128)}) custom-call(bf16[1,256,2560]{2,1,0:T(8,128)(2,1)} %get-tuple-element.229.attn, bf16[1,256,5120]{2,1,0:T(8,128)(2,1)} %get-tuple-element.230.resid, bf16[1,256,5120]{2,1,0:T(8,128)(2,1)} %get-tuple-element.231.cotan, ...), custom_call_target="tpu_custom_call" | custom-call | tf_op jit(solution)/shard_map/cond/branch_2_fun/step_2/pallas_call | solution.py:476
  252.6 0.0 copy-start
  252.6 4.0 %copy.78 = f32[1,320,2560]{2,1,0:T(8,128)} copy(f32[1,320,2560]{2,1,0:T(8,128)} %get-tuple-element.264) | data formatting | bytes 6553600
  256.6 0.0 copy-done
  256.6 0.0 copy-start.1
  256.6 1.7 copy.79
  258.4 1.4 copy-done.1
  259.8 1.7 copy.80
  (2 shorter events, 0.0 us)
Async XLA Ops:
  252.6 4.0 %copy-start = (f32[1,320,2560]{2,1,0:T(8,128)S(1)}, f32[1,320,2560]{2,1,0:T(8,128)}, u32[]{:S(2)}) copy-start(f32[1,320,2560]{2,1,0:T(8,128)} %get-tuple-element.265) | copy-start | bytes 9830404
  256.6 3.1 %copy-start.1 = (f32[1,320,2560]{2,1,0:T(8,128)S(1)}, f32[1,320,2560]{2,1,0:T(8,128)}, u32[]{:S(2)}) copy-start(f32[1,320,2560]{2,1,0:T(8,128)} %get-tuple-element.266) | copy-start | bytes 9830404

commit v2 on v1

--- a/solution.py
+++ b/solution.py
@@ -121,31 +121,28 @@
             dev(y, chip, core),
         )
 
-    routes = [
-        (place, rel, which)
-        for place in (2, 1, 3, 0)
-        for rel in range(2)
-        for which in range(2)
-        if place or rel
-    ]
+    near_routes = [(p, rel, which) for p in (2, 1) for rel in range(2) for which in range(2)]
+    near_routes += [(0, 1, 0), (0, 1, 1)]
+    far_routes = [(3, rel, which) for rel in range(2) for which in range(2)]
 
     def send_tokens(s):
         for order in range(3):
             tokens_copy(s, order).start()
         own_load(s, 2).start()
 
-    def send_features(s):
-        for route in routes:
+    def send_near_features(s):
+        for route in near_routes:
             features_copy(s, *route).start()
         own_load(s, 0).start()
         own_load(s, 1).start()
 
+    def send_far_features(s):
+        for route in far_routes:
+            features_copy(s, *route).start()
+
     send_tokens(0)
-    send_tokens(1)
-    send_features(0)
-    pf_copy = remote(params.at[0], pf_v, pf_ss, pf_rs, peer)
-    pf_copy.start()
-
+    send_near_features(0)
+    send_far_features(0)
     load_p.wait()
     step = 64 if shard % 64 == 0 else shard
 
@@ -177,6 +174,8 @@
             d = pl.ds(pl.multiple_of(c * shard + i * step, step), step)
             w_v[d, :] = w_s[r, :]
 
+    pf_copy = remote(params.at[0], pf_v, pf_ss, pf_rs, peer)
+    pf_copy.start()
     load_m.start()
     load_v.start()
 
@@ -199,20 +198,30 @@
         dst = attn_v.at[rows(s, chips[place], c, part)]
         return remote(dst, dst, rel_ss.at[s, part], attn_rs.at[s, 3, 0, part], device)
 
-    def issue(s):
+    def pass_on(s):
         arrival(s, 2, 0).wait_recv()
         relay(s, 0).start()
         arrival(s, 1, 0).wait_recv()
         relay(s, 1).start()
         forward(s, 1).start()
         forward(s, 2).start()
-        if s + 2 < N_PH:
-            send_tokens(s + 2)
-            send_features(s + 1)
-        elif s + 1 == N_PH:
-            send_features(s)
-
-    issue(0)
+
+    def collect(s):
+        own_load(s, 2).wait()
+        for part in range(2):
+            arrival(s, 3, 0, part).wait_recv()
+            forward(s, 3, part).start()
+        for place in range(3):
+            arrival(s, place, 1).wait_recv()
+        for part in range(2):
+            arrival(s, 3, 1, part).wait_recv()
+
+    pass_on(0)
+    send_tokens(1)
+    collect(0)
+    send_near_features(1)
+    send_far_features(1)
+    pass_on(1)
 
     def w_arrival(core):
         return remote(
@@ -247,23 +256,14 @@
             other,
         )
 
-    @pl.loop(0, N_PH)
-    def _(t):
-        for s in range(N_PH):
+    def matmul_and_sums(t):
+        for s in range(1, N_PH):
 
             @pl.when(t == s)
             def _():
-                if s + 1 < N_PH:
-                    issue(s + 1)
-                own_load(s, 2).wait()
-                arrival(s, 0, 1).wait_recv()
-                arrival(s, 1, 1).wait_recv()
-                arrival(s, 2, 1).wait_recv()
-                for part in range(2):
-                    arrival(s, 3, 0, part).wait_recv()
-                    forward(s, 3, part).start()
-                for part in range(2):
-                    arrival(s, 3, 1, part).wait_recv()
+                collect(s)
+                if s == 2:
+                    send_near_features(3)
 
         @pl.when(t == 0)
         def _():
@@ -282,13 +282,17 @@
             preferred_element_type=jnp.float32,
         )
 
+        @pl.when(t == 1)
+        def _():
+            pass_on(2)
+
         for s in range(N_PH):
 
             @pl.when(t == s)
             def _():
                 own_load(s, 0).wait()
                 own_load(s, 1).wait()
-                for place, rel, which in routes:
+                for place, rel, which in near_routes + far_routes:
                     block = (res_v, cot_v)[which].at[rows(s, chips[place], oc if rel else c)]
                     remote(
                         block,
@@ -311,11 +315,29 @@
             cross = jnp.sum(pre * scaled, axis=1, keepdims=True)
             sums_v[r, :] = jnp.where(lane == 0, square, cross)
 
-        part_sums = sums_v[...].T[0:2, :]
-        st_s[t] = part_sums
+        st_s[t] = sums_v[...].T[0:2, :]
         for k in range(1, N_ROW):
             st_copy(t, k).start()
-        total = part_sums
+
+        @pl.when(t == 0)
+        def _():
+            send_tokens(2)
+            send_near_features(2)
+
+        @pl.when(t == 1)
+        def _():
+            send_far_features(2)
+            send_tokens(3)
+
+        @pl.when(t == 2)
+        def _():
+            pass_on(3)
+            send_far_features(3)
+
+    def gradient_part(t):
+        base = pl.multiple_of(t * pair, pair)
+        gain = gain_r[0, 0:1, :] + gain_r[1, 0:1, :]
+        total = st_s[t]
         for k in range(1, N_ROW):
             st_copy(t, k).wait_recv()
             total = total + st_r[t, k]
@@ -353,6 +375,16 @@
                 gs_v[j] = acc[j].astype(jnp.bfloat16)
                 far_copy(j, 0).start()
                 far_copy(j, 1).start()
+
+    @pl.loop(0, N_PH + 1)
+    def _(t):
+        @pl.when(t > 0)
+        def _():
+            gradient_part(t - 1)
+
+        @pl.when(t < N_PH)
+        def _():
+            matmul_and_sums(t)
 
     load_m.wait()
     load_v.wait()
@@ -424,7 +456,7 @@
     for s in range(N_PH):
         for order in range(3):
             tokens_copy(s, order).wait_send()
-        for route in routes:
+        for route in near_routes + far_routes:
             features_copy(s, *route).wait_send()
         for part in range(2):
             relay(s, part).wait_send()

time: 262 us -> 177 us (0.68)
  Pallas kernels: 249 us -> 165 us
    pallas_call x1, Pallas kernels: 249 us -> 165 us  [run_step(): pl.pallas_call(functools.partial(step_kernel, bit), out_shape=(out, out,...]
where the time goes in v2:
time: 177 us
  Pallas kernels  165 us (93%)
  local copies, waits for them, and re-layouts  8.83 us (5%)
    pallas_call x1, Pallas kernels, run_step(): pl.pallas_call(functools.partial(step_kernel, bit), out_shape=(out, out,...  165 us
    unnamed x7, local copies, waits for them, and re-layouts  8.82 us

profile of v2, /device:TPU:1, one launch (start us, length us, event | category | flops | bytes accessed | tf_op | source)
XLA Modules:
  0.0 177.0 jit_solution(15317815535672972379)
XLA Ops:
  1.5 0.1 pad_maximum_fusion
  1.5 0.8 maximum_convert_fusion
  2.4 165.8 %conditional.1 = ((f32[1,320,2560]{2,1,0:T(8,128)}, f32[1,320,2560]{2,1,0:T(8,128)}, f32[1,320,2560]{2,1,0:T(8,128)})) conditional(s32[]{:T(128)} %clamp.3, (bf16[1,256,2560]{2,1,0:T(8,128)(2,1)}, bf16[1,256,5120]{2,1,0:T(8,128)(2,1)}, bf16[1,256,5120]{2,1,0:T(8,128)(2,1)}, s32[640]{0:T(1024)S(1)}, ...), branch_computations={%region_0.1_spmd.clone, %region_1.2_spmd.clone, %region_2.3_spmd.c... | conditional | flops 6402 | bytes 26913 | solution.py:592
  2.4 0.6 broadcast_select_fusion.gain_in
  3.0 165.0 %step_0.1 = (f32[1,320,2560]{2,1,0:T(8,128)}, f32[1,320,2560]{2,1,0:T(8,128)}, f32[1,320,2560]{2,1,0:T(8,128)}) custom-call(bf16[1,256,2560]{2,1,0:T(8,128)(2,1)} %get-tuple-element.175.attn, bf16[1,256,5120]{2,1,0:T(8,128)(2,1)} %get-tuple-element.176.resid, bf16[1,256,5120]{2,1,0:T(8,128)(2,1)} %get-tuple-element.177.cotan, ...), custom_call_target="tpu_custom_call" | custom-call | tf_op jit(solution)/shard_map/cond/branch_0_fun/step_0/pallas_call | solution.py:508
  168.2 0.0 copy-start
  168.2 4.0 %copy.78 = f32[1,320,2560]{2,1,0:T(8,128)} copy(f32[1,320,2560]{2,1,0:T(8,128)} %get-tuple-element.264) | data formatting | bytes 6553600
  172.2 0.0 copy-done
  172.2 0.0 copy-start.1
  172.2 1.7 copy.79
  173.9 1.4 copy-done.1
  175.3 1.7 copy.80
  (2 shorter events, 0.0 us)
Async XLA Ops:
  168.2 4.0 %copy-start = (f32[1,320,2560]{2,1,0:T(8,128)S(1)}, f32[1,320,2560]{2,1,0:T(8,128)}, u32[]{:S(2)}) copy-start(f32[1,320,2560]{2,1,0:T(8,128)} %get-tuple-element.265) | copy-start | bytes 9830404
  172.2 3.1 %copy-start.1 = (f32[1,320,2560]{2,1,0:T(8,128)S(1)}, f32[1,320,2560]{2,1,0:T(8,128)}, u32[]{:S(2)}) copy-start(f32[1,320,2560]{2,1,0:T(8,128)} %get-tuple-element.266) | copy-start | bytes 9830404

commit v3 on v2

--- a/solution.py
+++ b/solution.py
@@ -34,12 +34,13 @@
 def step_kernel(
     bit,
     attn, resid, cotan, gain_in, params, first_in, second_in, fixes,
-    params_out, first_out, second_out,
+    p_out, first_out, second_out,
     attn_v, res_v, cot_v, w_v, w_s, gain_r, pre_v, gp_v, acc, sums_v, inv_v, cor_v, st_s, st_r,
-    gs_v, near_v, far_v, p_v, pf_v, m_v, v_v, us_v, uf_v,
+    gs_v, near_v, far_v, pf_v, m_v, v_v, us_v, uf_v,
     own_sem, loc_sem, attn_ss, attn_rs, fwd_ss, rel_ss, a2a_ss, a2a_rs, w_ss, w_rs, g_ss, g_rs,
     pf_ss, pf_rs, st_ss, st_rs, far_ss, far_rs, near_ss, near_rs, u_ss, u_rs, out_sem,
 ):
+    p_v = p_out.at[0]
     tokens = attn.shape[1]
     piece = tokens // N_PH
     half = piece // 2
@@ -48,6 +49,7 @@
     shard = params.shape[1]
     feats = 2 * shard
     n_chunk, _, chunk = acc.shape
+    group = 4 if n_chunk % 4 == 0 else 1
 
     rep = lax.axis_index("rep")
     me = lax.axis_index("fsdp")
@@ -256,7 +258,7 @@
             other,
         )
 
-    def matmul_and_sums(t):
+    def first_matmul(t):
         for s in range(1, N_PH):
 
             @pl.when(t == s)
@@ -275,7 +277,7 @@
                     g_arrival(core).wait_recv()
 
         base = pl.multiple_of(t * pair, pair)
-        pre_v[...] = lax.dot_general(
+        pre_v[lax.rem(t, 2)] = lax.dot_general(
             attn_v[pl.ds(base, pair), :],
             w_v[...],
             (((1,), (1,)), ((), ())),
@@ -285,6 +287,10 @@
         @pl.when(t == 1)
         def _():
             pass_on(2)
+
+    def row_sums(t):
+        slot = lax.rem(t, 2)
+        base = pl.multiple_of(t * pair, pair)
 
         for s in range(N_PH):
 
@@ -308,8 +314,8 @@
         def _(i):
             r = pl.ds(pl.multiple_of(i * 64, 64), 64)
             b = pl.ds(pl.multiple_of(base + i * 64, 64), 64)
-            pre = pre_v[r, :] + res_v[b, :].astype(jnp.float32)
-            pre_v[r, :] = pre
+            pre = pre_v[slot, r, :] + res_v[b, :].astype(jnp.float32)
+            pre_v[slot, r, :] = pre
             scaled = gain * cot_v[b, :].astype(jnp.float32)
             square = jnp.sum(pre * pre, axis=1, keepdims=True)
             cross = jnp.sum(pre * scaled, axis=1, keepdims=True)
@@ -335,6 +341,7 @@
             send_far_features(3)
 
     def gradient_part(t):
+        slot = lax.rem(t, 2)
         base = pl.multiple_of(t * pair, pair)
         gain = gain_r[0, 0:1, :] + gain_r[1, 0:1, :]
         total = st_s[t]
@@ -356,35 +363,44 @@
             for k in range(feats // 128):
                 f = slice(k * 128, (k + 1) * 128)
                 scaled = gain[:, f] * cot_v[b, f].astype(jnp.float32)
-                grad_pre = (inv * scaled - pre_v[r, f] * cor).astype(jnp.bfloat16)
+                grad_pre = (inv * scaled - pre_v[slot, r, f] * cor).astype(jnp.bfloat16)
                 gp_v[f, r] = grad_pre.T
 
-        @pl.loop(0, n_chunk)
-        def _(j):
-            q = pl.ds(pl.multiple_of(j * chunk, chunk), chunk)
-            acc[j] += jnp.dot(
+        @pl.loop(0, n_chunk // group)
+        def _(i):
+            q = pl.ds(pl.multiple_of(i * group * chunk, group * chunk), group * chunk)
+            product = jnp.dot(
                 gp_v[...], attn_v[pl.ds(base, pair), q], preferred_element_type=jnp.float32
             )
+            for k in range(group):
+                acc[i * group + k] += product[:, k * chunk : (k + 1) * chunk]
 
             @pl.when(jnp.logical_and(t == N_PH - 1, keeper))
             def _():
-                near_copy(j).start()
+                for k in range(group):
+                    near_copy(i * group + k).start()
 
             @pl.when(jnp.logical_and(t == N_PH - 1, jnp.logical_not(keeper)))
             def _():
-                gs_v[j] = acc[j].astype(jnp.bfloat16)
-                far_copy(j, 0).start()
-                far_copy(j, 1).start()
+                for k in range(group):
+                    j = i * group + k
+                    gs_v[j] = acc[j].astype(jnp.bfloat16)
+                    far_copy(j, 0).start()
+                    far_copy(j, 1).start()
 
     @pl.loop(0, N_PH + 1)
     def _(t):
+        @pl.when(t < N_PH)
+        def _():
+            first_matmul(t)
+
         @pl.when(t > 0)
         def _():
             gradient_part(t - 1)
 
         @pl.when(t < N_PH)
         def _():
-            matmul_and_sums(t)
+            row_sums(t)
 
     load_m.wait()
     load_v.wait()
@@ -394,9 +410,13 @@
     def u_copy(j):
         return remote(us_v.at[j], uf_v.at[j], u_ss.at[j], u_rs.at[j], peer)
 
-    def out_copy(which, src, dst, j):
+    def out_copy(which, j):
         q = pl.ds(pl.multiple_of(j * chunk, chunk), chunk)
-        return pltpu.make_async_copy(src.at[:, q], dst.at[0, :, q], out_sem.at[which, j])
+        return pltpu.make_async_copy(
+            (m_v, v_v)[which].at[:, q],
+            (first_out, second_out)[which].at[0, :, q],
+            out_sem.at[which, j],
+        )
 
     def finish(j):
         q = pl.ds(pl.multiple_of(j * chunk, chunk), chunk)
@@ -407,9 +427,7 @@
             r = pl.ds(pl.multiple_of(i * step, step), step)
             p_v[r, q] = pf_v[r, q] + 0.5 * uf_v[j, r, :].astype(jnp.float32)
 
-        out_copy(0, p_v, params_out, j).start()
-
-    lag = min(2, n_chunk)
+    lag = min(6, n_chunk)
 
     @pl.loop(0, n_chunk)
     def _(j):
@@ -425,9 +443,9 @@
 
         far_copy(j, 0).wait_recv()
 
-        @pl.loop(0, shard // step)
+        @pl.loop(0, 2)
         def _(i):
-            r = pl.ds(pl.multiple_of(i * step, step), step)
+            r = pl.ds(pl.multiple_of(i * (shard // 2), shard // 2), shard // 2)
             gradient = near_v[j, r, :] + far_v[j, r, :].astype(jnp.float32)
             p = p_v[r, q]
             first_new = beta_one * m_v[r, q] + (1.0 - beta_one) * gradient
@@ -442,8 +460,8 @@
             pf_v[r, q] = 0.5 * (pf_v[r, q] - p) + 0.5 * update
 
         u_copy(j).start()
-        out_copy(1, m_v, first_out, j).start()
-        out_copy(2, v_v, second_out, j).start()
+        out_copy(0, j).start()
+        out_copy(1, j).start()
 
         @pl.when(j >= lag)
         def _():
@@ -489,9 +507,8 @@
             far_copy(j, 1).wait_send()
 
         u_copy(j).wait_send()
-        out_copy(0, p_v, params_out, j).wait()
-        out_copy(1, m_v, first_out, j).wait()
-        out_copy(2, v_v, second_out, j).wait()
+        out_copy(0, j).wait()
+        out_copy(1, j).wait()
 
 
 def run_step(attn, resid, cotan, gain_in, params, first, second, fixes, *, bit):
@@ -499,10 +516,10 @@
     shard = params.shape[1]
     feats, row = 2 * shard, N_ROW * tokens
     pair = row // N_PH
-    chunk = 256 if heads % 256 == 0 and heads > 256 else 128
+    chunk = 128
     n_chunk = heads // chunk
     bf16, f32, dma = jnp.bfloat16, jnp.float32, pltpu.SemaphoreType.DMA
-    any_spec = pl.BlockSpec(memory_space=pl.ANY)
+    any_spec = pl.BlockSpec(memory_space=pltpu.HBM)
     vmem = pltpu.VMEM
     out = jax.ShapeDtypeStruct(params.shape, f32)
     return pl.pallas_call(
@@ -518,7 +535,7 @@
             any_spec,
             pl.BlockSpec(memory_space=pltpu.SMEM),
         ],
-        out_specs=(any_spec, any_spec, any_spec),
+        out_specs=(pl.BlockSpec(memory_space=pltpu.VMEM), any_spec, any_spec),
         scratch_shapes=[
             vmem((row, heads), bf16),
             vmem((row, feats), bf16),
@@ -526,7 +543,7 @@
             vmem((feats, heads), bf16),
             vmem((shard, heads), bf16),
             vmem((2, 8, feats), f32),
-            vmem((pair, feats), f32),
+            vmem((2, pair, feats), f32),
             vmem((feats, pair), bf16),
             vmem((n_chunk, feats, chunk), f32),
             vmem((pair, 128), f32),
@@ -537,7 +554,6 @@
             vmem((n_chunk, feats, chunk), bf16),
             vmem((n_chunk, shard, chunk), f32),
             vmem((n_chunk, shard, chunk), bf16),
-            vmem((shard, heads), f32),
             vmem((shard, heads), f32),
             vmem((shard, heads), f32),
             vmem((shard, heads), f32),
@@ -565,12 +581,12 @@
             dma((n_chunk,)),
             dma((n_chunk,)),
             dma((n_chunk,)),
-            dma((3, n_chunk)),
+            dma((2, n_chunk)),
         ],
         compiler_params=pltpu.CompilerParams(
             collective_id=bit,
             has_side_effects=True,
-            vmem_limit_bytes=63 * 2**20,
+            vmem_limit_bytes=54 * 2**20,
         ),
         name=f"step_{bit}",
     )(attn, resid, cotan, gain_in, params, first, second, fixes)

time: 177 us -> 173 us (0.977)
  Pallas kernels: 165 us -> 160 us
    pallas_call x1, Pallas kernels: 165 us -> 160 us  [run_step(): pl.pallas_call(functools.partial(step_kernel, bit), out_shape=(out, out,...]
where the time goes in v3:
time: 173 us; the launch traced here: 171 us
  Pallas kernels  160 us (92%)
  local copies, waits for them, and re-layouts  7.92 us (5%)
    pallas_call x1, Pallas kernels, run_step(): pl.pallas_call(functools.partial(step_kernel, bit), out_shape=(out, out,...  160 us
    unnamed x7, local copies, waits for them, and re-layouts  7.92 us

profile of v3, /device:TPU:1, one launch (start us, length us, event | category | flops | bytes accessed | tf_op | source)
XLA Modules:
  0.0 171.4 jit_solution(9302445871370506856)
XLA Ops:
  1.5 0.1 pad_maximum_fusion
  1.5 0.8 maximum_convert_fusion
  2.4 161.1 %conditional.1 = ((f32[1,320,2560]{2,1,0:T(8,128)S(1)}, f32[1,320,2560]{2,1,0:T(8,128)}, f32[1,320,2560]{2,1,0:T(8,128)})) conditional(s32[]{:T(128)} %clamp.3, (bf16[1,256,2560]{2,1,0:T(8,128)(2,1)}, bf16[1,256,5120]{2,1,0:T(8,128)(2,1)}, bf16[1,256,5120]{2,1,0:T(8,128)(2,1)}, s32[640]{0:T(1024)S(1)}, ...), branch_computations={%region_0.1_spmd.clone, %region_1.2_spmd.clone, %region_2.3_spmd.c... | conditional | flops 6402 | bytes 26913 | solution.py:608
  2.4 0.6 broadcast_select_fusion.gain_in
  3.0 160.2 %step_0.1 = (f32[1,320,2560]{2,1,0:T(8,128)S(1)}, f32[1,320,2560]{2,1,0:T(8,128)}, f32[1,320,2560]{2,1,0:T(8,128)}) custom-call(bf16[1,256,2560]{2,1,0:T(8,128)(2,1)} %get-tuple-element.175.attn, bf16[1,256,5120]{2,1,0:T(8,128)(2,1)} %get-tuple-element.176.resid, bf16[1,256,5120]{2,1,0:T(8,128)(2,1)} %get-tuple-element.177.cotan, ...), custom_call_target="tpu_custom_call" | custom-call | tf_op jit(solution)/shard_map/cond/branch_0_fun/step_0/pallas_call | solution.py:525
  163.4 0.0 copy-start
  163.5 1.7 copy.78
  165.2 1.4 copy-done
  166.6 0.0 copy-start.1
  166.6 1.7 copy.79
  168.3 1.4 copy-done.1
  169.7 1.7 copy.80
  (2 shorter events, 0.0 us)
Async XLA Ops:
  163.4 3.1 %copy-start = (f32[1,320,2560]{2,1,0:T(8,128)S(1)}, f32[1,320,2560]{2,1,0:T(8,128)}, u32[]{:S(2)}) copy-start(f32[1,320,2560]{2,1,0:T(8,128)} %get-tuple-element.265) | copy-start | bytes 9830404
  166.6 3.1 %copy-start.1 = (f32[1,320,2560]{2,1,0:T(8,128)S(1)}, f32[1,320,2560]{2,1,0:T(8,128)}, u32[]{:S(2)}) copy-start(f32[1,320,2560]{2,1,0:T(8,128)} %get-tuple-element.266) | copy-start | bytes 9830404

commit v4 on v3

--- a/solution.py
+++ b/solution.py
@@ -132,11 +132,13 @@
             tokens_copy(s, order).start()
         own_load(s, 2).start()
 
-    def send_near_features(s):
-        for route in near_routes:
-            features_copy(s, *route).start()
-        own_load(s, 0).start()
-        own_load(s, 1).start()
+    def send_near_features(s, parts=(0, 1)):
+        for place, rel, which in near_routes:
+            if (which if place else 1) in parts:
+                features_copy(s, place, rel, which).start()
+        if 1 in parts:
+            own_load(s, 0).start()
+            own_load(s, 1).start()
 
     def send_far_features(s):
         for route in far_routes:
@@ -265,7 +267,7 @@
             def _():
                 collect(s)
                 if s == 2:
-                    send_near_features(3)
+                    send_near_features(3, (0,))
 
         @pl.when(t == 0)
         def _():
@@ -308,7 +310,7 @@
                         other,
                     ).wait_recv()
 
-        gain = gain_r[0, 0:1, :] + gain_r[1, 0:1, :]
+        gain = jnp.concatenate([gain_r[0, 0:1, :], gain_r[1, 0:1, :]], axis=1)
 
         @pl.loop(0, pair // 64)
         def _(i):
@@ -338,12 +340,13 @@
         @pl.when(t == 2)
         def _():
             pass_on(3)
+            send_near_features(3, (1,))
             send_far_features(3)
 
     def gradient_part(t):
         slot = lax.rem(t, 2)
         base = pl.multiple_of(t * pair, pair)
-        gain = gain_r[0, 0:1, :] + gain_r[1, 0:1, :]
+        gain = jnp.concatenate([gain_r[0, 0:1, :], gain_r[1, 0:1, :]], axis=1)
         total = st_s[t]
         for k in range(1, N_ROW):
             st_copy(t, k).wait_recv()
@@ -542,7 +545,7 @@
             vmem((row, feats), bf16),
             vmem((feats, heads), bf16),
             vmem((shard, heads), bf16),
-            vmem((2, 8, feats), f32),
+            vmem((2, 8, shard), f32),
             vmem((2, pair, feats), f32),
             vmem((feats, pair), bf16),
             vmem((n_chunk, feats, chunk), f32),
@@ -597,11 +600,7 @@
     first_fix = 1.0 - jnp.power(jnp.float32(beta_one), step_time)
     second_fix = 1.0 - jnp.power(jnp.float32(beta_two), step_time)
     fixes = jnp.stack([1.0 / first_fix, 1.0 / second_fix])
-    shard = norm_gain.shape[0]
-    core = lax.rem(lax.axis_index("fsdp"), 2)
-    gain = norm_gain.astype(jnp.float32)
-    owner = lax.div(lax.broadcasted_iota(jnp.int32, (8, 2 * shard), 1), shard)
-    gain_in = jnp.where(owner == core, jnp.concatenate([gain, gain])[None, :], 0.0)
+    gain_in = jnp.broadcast_to(norm_gain.astype(jnp.float32)[None, :], (8, norm_gain.shape[0]))
     level_count = lax.axis_size("rep").bit_length() - 1
     level = jnp.remainder(step_count[0], level_count)
     branches = [functools.partial(run_step, bit=bit) for bit in range(level_count)]

time: 173 us -> 204 us (1.18)
  Pallas kernels: 160 us -> 192 us
    pallas_call x1, Pallas kernels: 160 us -> 192 us  [run_step(): pl.pallas_call(functools.partial(step_kernel, bit), out_shape=(out, out,...]
where the time goes in v4:
time: 204 us; the launch traced here: 203 us
  Pallas kernels  192 us (94%)
  local copies, waits for them, and re-layouts  8.52 us (4%)
    pallas_call x1, Pallas kernels, run_step(): pl.pallas_call(functools.partial(step_kernel, bit), out_shape=(out, out,...  192 us
    unnamed x7, local copies, waits for them, and re-layouts  7.92 us

profile of v4, /device:TPU:1, one launch (start us, length us, event | category | flops | bytes accessed | tf_op | source)
XLA Modules:
  0.0 203.3 jit_solution(10463464765282216444)
XLA Ops:
  1.5 0.1 pad_maximum_fusion
  1.5 0.7 convert_element_type.7
  2.2 193.1 %conditional.1 = ((f32[1,320,2560]{2,1,0:T(8,128)S(1)}, f32[1,320,2560]{2,1,0:T(8,128)}, f32[1,320,2560]{2,1,0:T(8,128)})) conditional(s32[]{:T(128)} %clamp.3, (bf16[1,256,2560]{2,1,0:T(8,128)(2,1)}, bf16[1,256,5120]{2,1,0:T(8,128)(2,1)}, bf16[1,256,5120]{2,1,0:T(8,128)(2,1)}, f32[320]{0:T(512)S(1)}, f32[1,320,2560]{2,1,0:T(8,128)}, ...), branch_computations={%region_0.1_spmd, %region_1.2_spmd, %region_2.3_spmd} | conditional | bytes 11528 | solution.py:607
  2.2 0.6 broadcast_in_dim.9.gain_in
  2.8 192.3 %step_2.1 = (f32[1,320,2560]{2,1,0:T(8,128)S(1)}, f32[1,320,2560]{2,1,0:T(8,128)}, f32[1,320,2560]{2,1,0:T(8,128)}) custom-call(bf16[1,256,2560]{2,1,0:T(8,128)(2,1)} %get-tuple-element.110.attn, bf16[1,256,5120]{2,1,0:T(8,128)(2,1)} %get-tuple-element.113.resid, bf16[1,256,5120]{2,1,0:T(8,128)(2,1)} %get-tuple-element.116.cotan, ...), custom_call_target="tpu_custom_call" | custom-call | tf_op jit(solution)/shard_map/cond/branch_2_fun/step_2/pallas_call | solution.py:528
  195.3 0.0 copy-start
  195.3 1.7 copy.51
  197.1 1.4 copy-done
  198.4 0.0 copy-start.1
  198.4 1.7 copy.52
  200.2 1.4 copy-done.1
  201.6 1.7 copy.53
Async XLA Ops:
  195.3 3.1 %copy-start = (f32[1,320,2560]{2,1,0:T(8,128)S(1)}, f32[1,320,2560]{2,1,0:T(8,128)}, u32[]{:S(2)}) copy-start(f32[1,320,2560]{2,1,0:T(8,128)} %get-tuple-element.139) | copy-start | bytes 9830404
  198.4 3.1 %copy-start.1 = (f32[1,320,2560]{2,1,0:T(8,128)S(1)}, f32[1,320,2560]{2,1,0:T(8,128)}, u32[]{:S(2)}) copy-start(f32[1,320,2560]{2,1,0:T(8,128)} %get-tuple-element.140) | copy-start | bytes 9830404
